TPU v7x, 512 devices: a whole 4x8x8 slice. The times are simulated.
512 devices in a mesh: sub: 16 (over z, core), tile: 32 (over y, x).
Axes of the slice: x: 4, y: 8, z: 8, core: 2. Of those that a mesh axis runs over, the one named last changes fastest.
Arguments:
- echoes: float32 [32, 32, 128], P('sub', 'tile'), may hold values from -6 to 6
- pulse_offset: float32 [32, 32], P('sub', 'tile'), may hold values from 0 to 1
- range_gates: int32 [32, 32, 64], P('sub', 'tile'), may hold values from 0 to 511
- visible: int32 [32, 256], P('sub', 'tile'), may hold values 0 or 1
Outputs:
- images: float32 [32, 256, 128, 256], P('sub', 'tile')
- peak: float32 [256, 128, 128], P('tile', 'sub')
All inputs are finite; a program needn't handle non-finite values. No bound on the sum of `visible` on one device may be relied on, other than what follows from the above.
Results may differ from a plain program's by a relative error of at most 0.0037.
Values sent between devices are 32-bit elements; how exact they have to be, the bound alone decides.
No kernel may reach another device: no remote copies, remote signals or barrier semaphores. Data moves between devices by JAX's collectives and lax.ppermute only.
A program may use at most 64 MiB of HBM per device.

v0:
```python
import math
import jax
import jax.numpy as jnp
from jax import lax
from jax.sharding import PartitionSpec as P

PULSE_H = 32
FREQS = 64
PIX = 128
GATES = 512
grid_cols = 16
two_pi = 2.0 * math.pi


def shifted(block, axis, distance):
    devices = range(lax.axis_size(axis))
    route = [((i - distance) % len(devices), i) for i in devices]
    return lax.ppermute(block, axis, route)


def make_right(sine_wave):
    pixels = jnp.arange(PIX, dtype=jnp.float32)
    phase_grid = sine_wave[:, None] * pixels[None, :]
    real_part = jnp.cos(phase_grid).astype(jnp.bfloat16)
    imag_part = jnp.sin(phase_grid).astype(jnp.bfloat16)
    upper = jnp.concatenate([real_part, imag_part], axis=1)
    lower = jnp.concatenate([-imag_part, real_part], axis=1)
    return jnp.concatenate([upper, lower], axis=0)


def make_base(cosine_wave):
    pixels = jnp.arange(PIX, dtype=jnp.float32)
    base_phase = cosine_wave[None, :] * pixels[:, None]
    return (jnp.cos(base_phase), jnp.sin(base_phase))


def make_left(
    echo_real, echo_imag, cosine_wave, sine_wave, base_cos, base_sin, tile_number, norm_scale
):
    column = (tile_number % grid_cols * PIX - 8 * PIX).astype(jnp.float32)
    row_start = (tile_number // grid_cols * PIX - 4 * PIX).astype(jnp.float32)
    offset_phase = cosine_wave * column + sine_wave * row_start
    offset_cos = jnp.cos(offset_phase)
    offset_sin = jnp.sin(offset_phase)
    turned_real = norm_scale * (echo_real * offset_cos - echo_imag * offset_sin)
    turned_imag = norm_scale * (echo_real * offset_sin + echo_imag * offset_cos)
    real_part = turned_real[None, :] * base_cos - turned_imag[None, :] * base_sin
    imag_part = turned_real[None, :] * base_sin + turned_imag[None, :] * base_cos
    return jnp.concatenate([real_part, imag_part], axis=1).astype(jnp.bfloat16)


def on_device(echoes, pulse_offset, range_gates, visible):
    half_dev = echoes.shape[0]
    tile_dev = visible.shape[1]
    sub_count = lax.axis_size("sub")
    half_total = half_dev * sub_count
    first_half = lax.axis_index("sub") * half_dev
    first_tile = lax.axis_index("tile") * tile_dev
    half_numbers = first_half + jnp.arange(half_dev, dtype=jnp.int32)
    angles = two_pi * (half_numbers.astype(jnp.float32)[:, None] + pulse_offset) / half_total
    waves = 0.5 + range_gates.astype(jnp.float32) / GATES
    shown = visible.astype(jnp.float32)
    half_count = echoes.shape[0]
    norm_scale = (2.0 * PULSE_H * FREQS) ** (-0.5)
    echo_piece = lax.all_gather(echoes, "tile", axis=1, tiled=True)
    wave_piece = lax.all_gather(waves, "tile", axis=1, tiled=True)
    angle_piece = lax.all_gather(angles, "tile", axis=1, tiled=True)
    stacked = []
    for half_slot in range(half_count):
        cosine_wave = (wave_piece[half_slot] * jnp.cos(angle_piece[half_slot])[:, None]).reshape(-1)
        sine_wave = (wave_piece[half_slot] * jnp.sin(angle_piece[half_slot])[:, None]).reshape(-1)
        echo_real = echo_piece[half_slot][:, :FREQS].reshape(-1)
        echo_imag = echo_piece[half_slot][:, FREQS:].reshape(-1)
        right_side = make_right(sine_wave)
        base_cos, base_sin = make_base(cosine_wave)
        tile_terms = []
        for tile_slot in range(tile_dev):

            def compute(
                echo_real=echo_real,
                echo_imag=echo_imag,
                cosine_wave=cosine_wave,
                sine_wave=sine_wave,
                base_cos=base_cos,
                base_sin=base_sin,
                right_side=right_side,
                tile_slot=tile_slot,
            ):
                left_side = make_left(
                    echo_real,
                    echo_imag,
                    cosine_wave,
                    sine_wave,
                    base_cos,
                    base_sin,
                    first_tile + tile_slot,
                    norm_scale,
                )
                return jnp.dot(left_side, right_side, preferred_element_type=jnp.float32)

            tile_term = compute()
            tile_terms.append(tile_term)
        stacked.append(jnp.stack(tile_terms))
    half_images = jnp.stack(stacked)
    half_images = half_images * shown[:, :, None, None]
    following = shifted(half_images[0], "sub", -1)
    successors = jnp.concatenate([half_images[1:half_dev], following[None]], axis=0)
    images = half_images + successors
    power_map = images[..., :PIX] ** 2 + images[..., PIX:] ** 2
    local_peak = jnp.max(power_map, axis=0)
    full_peak = lax.pmax(local_peak, "sub")
    row_count = PIX // sub_count
    peak = lax.dynamic_slice_in_dim(full_peak, lax.axis_index("sub") * row_count, row_count, 1)
    return (images, peak)


def solution(mesh):
    in_specs = (P("sub", "tile", None), P("sub", "tile"), P("sub", "tile", None), P("sub", "tile"))
    out_specs = (P("sub", "tile", None, None), P("tile", "sub", None))
    return jax.shard_map(
        on_device, mesh=mesh, in_specs=in_specs, out_specs=out_specs, check_vma=False
    )
```

profile of v0, /device:TPU:1, one launch (start us, length us, event | category | flops | bytes accessed | tf_op | source)
XLA Modules:
  0.0 301.1 jit_solution(487523907034118992)
XLA Ops:
  7.2 0.0 all-reduce.2.cloned.1.call-start
  7.3 0.7 multiply_bitcast_fusion
  8.0 29.8 %all-gather = f32[32,1,2]{2,1,0:T(1,128)S(1)} all-gather(f32[1,1,2]{2,1,0:T(1,128)S(1)} %multiply_bitcast_fusion), channel_id=1, replica_groups=mesh['sub'=16,'tile'=32] {'tile'}, dimensions={0}, use_global_device_ids=true | all-gather | bytes 264 | tf_op jit(solution)/shard_map/all_gather | solution.py:67
  37.8 0.1 copy.9
  37.9 0.1 sine_bitcast_fusion.1
  37.9 0.1 mul.1893
  38.0 0.1 mul.1894
  38.1 0.1 mul.1900
  38.1 0.1 mul.1901
  38.2 0.1 mul.2050
  38.3 0.1 mul.2051
  38.3 0.1 mul.2054
  38.4 0.1 mul.2055
  38.5 29.0 %all_gather.9 = f32[2,32,128]{2,0,1:T(2,128)S(1)} all-gather(f32[2,1,128]{2,0,1:T(2,128)} %bitcast.94), channel_id=1, replica_groups=mesh['sub'=16,'tile'=32] {'tile'}, dimensions={1}, use_global_device_ids=true | all-gather | bytes 33792 | tf_op jit(solution)/shard_map/all_gather | solution.py:65
  67.5 0.1 fusion.122
  67.6 0.1 reshape.961
  67.6 0.1 reshape.962
  67.7 0.1 fusion.123
  67.8 0.1 reshape.963
  67.9 0.1 reshape.964
  67.9 0.7 multiply_add_fusion.16
  68.6 28.6 %all_gather.10 = f32[2,32,64]{2,0,1:T(2,128)S(1)} all-gather(f32[2,1,64]{2,0,1:T(2,128)S(1)} %multiply_add_fusion.16), channel_id=1, replica_groups=mesh['sub'=16,'tile'=32] {'tile'}, dimensions={1}, use_global_device_ids=true | all-gather | bytes 16896 | tf_op jit(solution)/shard_map/all_gather | solution.py:66
  97.2 0.1 slice_reduce_fusion.1
  97.3 0.1 squeeze.11
  97.4 0.1 squeeze.26
  97.4 0.1 subtract_multiply_fusion
  97.5 4.5 %sine_convert_fusion.1 = (bf16[2048,128]{1,0:T(8,128)(2,1)S(1)}, bf16[2048,128]{1,0:T(8,128)(2,1)S(1)}) fusion(f32[2048]{0:T(1024)S(1)} %get-tuple-element.117), kind=kLoop, calls=%fused_computation.125 | loop fusion | flops 786432 | bytes 1056768 | tf_op jit(solution)/shard_map/convert_element_type | solution.py:25
  102.0 4.1 %fusion.70 = bf16[2048,128]{1,0:T(8,128)(2,1)S(1)} fusion(f32[2048]{0:T(1024)S(1)} %get-tuple-element.117), kind=kLoop, calls=%fused_computation.133 | loop fusion | flops 1310720 | bytes 532480 | tf_op jit(solution)/shard_map/neg | solution.py:27
  106.2 0.1 subtract_multiply_fusion.15
  106.2 0.1 subtract_multiply_fusion.7
  106.3 0.3 add_multiply_fusion.8
  106.6 0.3 add_multiply_fusion
  106.8 4.5 %sine_convert_fusion = (bf16[2048,128]{1,0:T(8,128)(2,1)S(1)}, bf16[2048,128]{1,0:T(8,128)(2,1)S(1)}) fusion(f32[2048]{0:T(1024)S(1)} %get-tuple-element.9), kind=kLoop, calls=%fused_computation.103 | loop fusion | flops 786432 | bytes 1056768 | tf_op jit(solution)/shard_map/convert_element_type | solution.py:25
  111.3 4.1 %fusion.71 = bf16[2048,128]{1,0:T(8,128)(2,1)S(1)} fusion(f32[2048]{0:T(1024)S(1)} %get-tuple-element.9), kind=kLoop, calls=%fused_computation.134 | loop fusion | flops 1310720 | bytes 532480 | tf_op jit(solution)/shard_map/neg | solution.py:27
  115.4 0.0 copy-done.1
  115.4 6.3 %subtract_convert_fusion.8 = (bf16[128,2048]{1,0:T(8,128)(2,1)S(1)}, bf16[128,2048]{1,0:T(8,128)(2,1)S(1)}, bf16[128,2048]{1,0:T(8,128)(2,1)S(1)}, bf16[128,2048...) fusion(f32[2048]{0:T(1024)S(1)} %get-tuple-element.12, ...), kind=kLoop, calls=%fused_computation.112 | loop fusion | flops 17039360 | bytes 8527872 | tf_op jit(solution)/shard_map/convert.16
  121.7 0.5 fusion.15
  122.2 0.5 fusion.14
  122.6 0.5 fusion.13
  123.1 0.5 fusion.12
  123.6 0.5 fusion.11
  124.1 0.5 fusion.10
  124.6 0.5 fusion.9
  125.1 0.5 fusion.8
  125.6 6.2 %subtract_convert_fusion = (bf16[128,2048]{1,0:T(8,128)(2,1)S(1)}, bf16[128,2048]{1,0:T(8,128)(2,1)S(1)}, bf16[128,2048]{1,0:T(8,128)(2,1)S(1)}, bf16[128,2048]{...) fusion(f32[2048]{0:T(1024)S(1)} %get-tuple-element.29, ...), kind=kLoop, calls=%fused_computation.90 | loop fusion | flops 17039360 | bytes 8527872 | tf_op jit(solution)/shard_map/convert
  131.8 0.4 fusion.7
  132.2 0.4 fusion.6
  132.7 0.4 fusion.5
  133.1 0.4 fusion.4
  133.6 0.4 fusion.3
  134.0 0.5 fusion.2
  134.5 0.5 fusion.1
  135.0 0.5 fusion
  135.5 0.3 maximum_multiply_fusion
  135.7 0.2 fusion.120
  135.9 25.8 %collective-permute-start = (f32[8,128,256]{2,1,0:T(8,128)S(1)}, f32[8,128,256]{2,1,0:T(8,128)S(1)}, u32[]{:S(2)}, u32[]{:S(2)}) collective-permute-start(f32[8,128,256]{2,1,0:T(8,128)S(1)} %get-tuple-element.11), channel_id=1, source_target_pairs={{32,0},{64,32},{96,64},{128,96},{160,128},{192,160},{224,192},{256... | collective-permute-start | bytes 3145736 | tf_op jit(solution)/shard_map/ppermute | solution.py:18
  161.7 13.5 %collective-permute-done = f32[8,128,256]{2,1,0:T(8,128)S(1)} collective-permute-done((f32[8,128,256]{2,1,0:T(8,128)S(1)}, f32[8,128,256]{2,1,0:T(8,128)S(1)}, u32[]{:S(2)}, u32[]{:S(2)}) %collective-permute-start) | collective-permute-done | bytes 1048608 | tf_op jit(solution)/shard_map/ppermute | solution.py:18
  175.2 0.3 maximum_add_fusion
  175.6 0.0 copy-start
  175.6 1.1 fusion.17
  176.7 0.0 all-reduce.2.cloned.1.call-update
  176.7 116.2 %all-reduce.2.cloned.1.call-done = f32[8,128,128]{2,1,0:T(8,128)} async-done(((f32[8,128,128]{2,1,0:T(8,128)}), f32[8,128,128]{2,1,0:T(8,128)}) %all-reduce.2.cloned.1.call-update) | async-done | bytes 524304 | tf_op jit(solution)/shard_map/pmax | solution.py:111
  292.9 1.4 constant_dynamic-slice_fusion
  294.3 0.0 copy-done
  (3 shorter events, 0.0 us)
Async XLA Ops:
  7.2 285.7 %all-reduce.2.cloned.1.call-start = ((), (), s32[]{:S(2)}) async-start(), calls=%async_computation | async-start | bytes 1048576 | tf_op jit(solution)/shard_map/pmax | solution.py:111
  67.7 47.7 %copy-start.1 = (s32[2,8]{1,0:T(2,128)S(1)}, s32[2,8]{1,0:T(2,128)}, u32[]{:S(2)}) copy-start(s32[2,8]{1,0:T(2,128)} %param.7) | copy-start | bytes 196
  135.9 39.3 %collective-permute-start = (f32[8,128,256]{2,1,0:T(8,128)S(1)}, f32[8,128,256]{2,1,0:T(8,128)S(1)}, u32[]{:S(2)}, u32[]{:S(2)}) collective-permute-start(f32[8,128,256]{2,1,0:T(8,128)S(1)} %get-tuple-element.11), channel_id=1, source_target_pairs={{32,0},{64,32},{96,64},{128,96},{160,128},{192,160},{224,192},{256... | collective-permute-start | bytes 3145736 | tf_op jit(solution)/shard_map/ppermute | solution.py:18
  175.6 118.7 %copy-start = (f32[2,8,128,256]{3,2,1,0:T(8,128)}, f32[2,8,128,256]{3,2,1,0:T(8,128)S(1)}, u32[]{:S(2)}) copy-start(f32[2,8,128,256]{3,2,1,0:T(8,128)S(1)} %maximum_add_fusion) | copy-start | bytes 6291460
Sparse Core Ops, SparseCore 0:
  176.8 116.0 all-reduce.1
where the time goes:
time: 301 us
  waiting for transfers between devices  130 us (43%)
  blocking collectives  87.4 us (29%)
  other arithmetic  33.3 us (11%)
  starting transfers between devices  25.8 us (9%)
  between operations  14.5 us (5%)
  matrix products  7.47 us (2%)
    pmax x1, waiting for transfers between devices, on_device(): full_peak = lax.pmax(local_peak, 'sub')  116 us
    all_gather x1, blocking collectives, on_device(): angle_piece = lax.all_gather(angles, 'tile', axis=1, tiled=True)  29.8 us
    all_gather x1, blocking collectives, on_device(): echo_piece = lax.all_gather(echoes, 'tile', axis=1, tiled=True)  29 us
    all_gather x1, blocking collectives, on_device(): wave_piece = lax.all_gather(waves, 'tile', axis=1, tiled=True)  28.6 us
    ppermute x1, starting transfers between devices, shifted(): return lax.ppermute(block, axis, route)  25.8 us
    ppermute x1, waiting for transfers between devices, shifted(): return lax.ppermute(block, axis, route)  13.5 us
    another operation x2, other arithmetic  12.5 us
    convert_element_type x2, other arithmetic, make_right(): imag_part = jnp.sin(phase_grid).astype(jnp.bfloat16)  8.92 us
  transfers between devices with their start and end apart: 2, of which 2 were waited for; matrix products, arithmetic and copies ran while one was open for 0% of the time, Pallas kernels for 0%

commit v1 on v0

--- a/solution.py
+++ b/solution.py
@@ -63,7 +63,15 @@
     half_count = echoes.shape[0]
     norm_scale = (2.0 * PULSE_H * FREQS) ** (-0.5)
     echo_piece = lax.all_gather(echoes, "tile", axis=1, tiled=True)
-    wave_piece = lax.all_gather(waves, "tile", axis=1, tiled=True)
+    wave_piece = jnp.concatenate(
+        lax.all_to_all(
+            jnp.stack(tuple((waves for _ in range(lax.axis_size("tile"))))),
+            split_axis=0,
+            concat_axis=0,
+            axis_name="tile",
+        ),
+        1,
+    )
     angle_piece = lax.all_gather(angles, "tile", axis=1, tiled=True)
     stacked = []
     for half_slot in range(half_count):

time: 301 us -> 278 us (0.924)
  blocking collectives: 87.4 us -> 57.9 us
    all_gather x1 -> x0, blocking collectives: 28.6 us -> none  [on_device(): wave_piece = lax.all_gather(waves, 'tile', axis=1, tiled=True)]
    all_to_all x0 -> x1, starting transfers between devices: none -> 10.5 us  [on_device(): lax.all_to_all(jnp.stack(tuple((waves for _ in range(lax.axis_size('tile'...]
    ppermute x1, starting transfers between devices: 25.8 us -> 16.7 us  [shifted(): return lax.ppermute(block, axis, route)]
    another operation x2 -> x3, other arithmetic: 12.5 us -> 13.3 us
  transfers between devices with their start and end apart: 2 -> 3, of which waited for: 2 -> 2; matrix products, arithmetic and copies ran while one was open for 0% -> 1% of each run, Pallas kernels for 0% -> 0%
where the time goes in v1:
time: 278 us
  waiting for transfers between devices  131 us (47%)
  blocking collectives  57.9 us (21%)
  other arithmetic  35.5 us (13%)
  starting transfers between devices  27.3 us (10%)
  between operations  14.4 us (5%)
  matrix products  7.69 us (3%)
  local copies, waits for them, and re-layouts  4.21 us (2%)
    pmax x1, waiting for transfers between devices, on_device(): full_peak = lax.pmax(local_peak, 'sub')  116 us
    all_gather x1, blocking collectives, on_device(): echo_piece = lax.all_gather(echoes, 'tile', axis=1, tiled=True)  29.1 us
    all_gather x1, blocking collectives, on_device(): angle_piece = lax.all_gather(angles, 'tile', axis=1, tiled=True)  28.8 us
    ppermute x1, starting transfers between devices, shifted(): return lax.ppermute(block, axis, route)  16.7 us
    ppermute x1, waiting for transfers between devices, shifted(): return lax.ppermute(block, axis, route)  14.5 us
    another operation x2, other arithmetic  12.6 us
    all_to_all x1, starting transfers between devices, on_device(): lax.all_to_all(jnp.stack(tuple((waves for _ in range(lax.axis_size('tile'...  10.5 us
    convert_element_type x2, other arithmetic, make_right(): imag_part = jnp.sin(phase_grid).astype(jnp.bfloat16)  8.92 us
  transfers between devices with their start and end apart: 3, of which 2 were waited for; matrix products, arithmetic and copies ran while one was open for 1% of the time, Pallas kernels for 0%

profile of v1, /device:TPU:1, one launch (start us, length us, event | category | flops | bytes accessed | tf_op | source)
XLA Modules:
  0.0 277.8 jit_solution(16509153993474741502)
XLA Ops:
  7.2 0.7 multiply_add_fusion.16
  7.9 0.5 broadcast.438
  8.4 0.7 reduce.8
  9.1 0.7 reshape.993
  9.8 10.5 %all-to-all-start = ((f32[32,1,128]{2,1,0:T(1,128)}), f32[32,1,128]{2,1,0:T(1,128)S(1)}, u32[]{:S(2)}, u32[]{:S(2)}) async-start(f32[32,1,128]{2,1,0:T(1,128)} %reshape.993), calls=%async_computation | async-start | bytes 32768 | tf_op jit(solution)/shard_map/all_to_all | solution.py:67
  20.4 0.7 multiply_bitcast_fusion
  21.0 28.8 %all-gather = f32[32,1,2]{2,1,0:T(1,128)S(1)} all-gather(f32[1,1,2]{2,1,0:T(1,128)S(1)} %multiply_bitcast_fusion), channel_id=1, replica_groups=mesh['sub'=16,'tile'=32] {'tile'}, dimensions={0}, use_global_device_ids=true | all-gather | bytes 264 | tf_op jit(solution)/shard_map/all_gather | solution.py:75
  49.9 0.1 copy.8
  49.9 29.1 %all_gather.6 = f32[2,32,128]{2,0,1:T(2,128)S(1)} all-gather(f32[2,1,128]{2,0,1:T(2,128)} %bitcast.97), channel_id=1, replica_groups=mesh['sub'=16,'tile'=32] {'tile'}, dimensions={1}, use_global_device_ids=true | all-gather | bytes 33792 | tf_op jit(solution)/shard_map/all_gather | solution.py:65
  79.1 0.1 fusion.122
  79.2 0.1 fusion.123
  79.4 0.1 mul.1893
  79.4 0.1 mul.1894
  79.5 0.1 mul.1900
  79.6 0.1 mul.1901
  79.7 0.1 mul.2050
  79.7 0.1 mul.2051
  79.8 0.1 mul.2054
  79.9 0.1 mul.2055
  79.9 0.1 reshape.972
  80.0 0.1 reshape.974
  80.1 0.1 reshape.975
  80.2 0.1 reshape.976
  80.2 0.7 convert_element_type.130
  80.9 0.7 reduce.9
  81.6 0.1 reshape.994
  81.7 0.1 slice_reduce_fusion.1
  81.8 0.1 squeeze.11
  81.9 0.1 squeeze.26
  81.9 0.1 subtract_multiply_fusion
  82.0 4.5 %sine_convert_fusion.1 = (bf16[2048,128]{1,0:T(8,128)(2,1)S(1)}, bf16[2048,128]{1,0:T(8,128)(2,1)S(1)}) fusion(f32[2048]{0:T(1024)S(1)} %get-tuple-element.117), kind=kLoop, calls=%fused_computation.125 | loop fusion | flops 786432 | bytes 1056768 | tf_op jit(solution)/shard_map/convert_element_type | solution.py:25
  86.5 4.1 %fusion.70 = bf16[2048,128]{1,0:T(8,128)(2,1)S(1)} fusion(f32[2048]{0:T(1024)S(1)} %get-tuple-element.117), kind=kLoop, calls=%fused_computation.133 | loop fusion | flops 1310720 | bytes 532480 | tf_op jit(solution)/shard_map/neg | solution.py:27
  90.6 0.1 subtract_multiply_fusion.15
  90.6 0.1 subtract_multiply_fusion.7
  90.7 0.3 add_multiply_fusion.8
  91.0 0.3 add_multiply_fusion
  91.2 4.5 %sine_convert_fusion = (bf16[2048,128]{1,0:T(8,128)(2,1)S(1)}, bf16[2048,128]{1,0:T(8,128)(2,1)S(1)}) fusion(f32[2048]{0:T(1024)S(1)} %get-tuple-element.9), kind=kLoop, calls=%fused_computation.103 | loop fusion | flops 786432 | bytes 1056768 | tf_op jit(solution)/shard_map/convert_element_type | solution.py:25
  95.7 4.1 %fusion.71 = bf16[2048,128]{1,0:T(8,128)(2,1)S(1)} fusion(f32[2048]{0:T(1024)S(1)} %get-tuple-element.9), kind=kLoop, calls=%fused_computation.134 | loop fusion | flops 1310720 | bytes 532480 | tf_op jit(solution)/shard_map/neg | solution.py:27
  99.8 6.3 %subtract_convert_fusion.8 = (bf16[128,2048]{1,0:T(8,128)(2,1)S(1)}, bf16[128,2048]{1,0:T(8,128)(2,1)S(1)}, bf16[128,2048]{1,0:T(8,128)(2,1)S(1)}, bf16[128,2048...) fusion(f32[2048]{0:T(1024)S(1)} %get-tuple-element.12, ...), kind=kLoop, calls=%fused_computation.112 | loop fusion | flops 17039360 | bytes 8527872 | tf_op jit(solution)/shard_map/convert.16
  106.1 0.5 fusion.15
  106.6 0.5 fusion.14
  107.1 0.5 fusion.13
  107.6 0.5 fusion.12
  108.0 0.5 fusion.11
  108.5 0.5 fusion.10
  109.0 0.5 fusion.9
  109.5 0.5 fusion.8
  110.0 6.3 %subtract_convert_fusion = (bf16[128,2048]{1,0:T(8,128)(2,1)S(1)}, bf16[128,2048]{1,0:T(8,128)(2,1)S(1)}, bf16[128,2048]{1,0:T(8,128)(2,1)S(1)}, bf16[128,2048]{...) fusion(f32[2048]{0:T(1024)S(1)} %get-tuple-element.29, ...), kind=kLoop, calls=%fused_computation.90 | loop fusion | flops 17039360 | bytes 8527872 | tf_op jit(solution)/shard_map/convert
  116.3 0.5 fusion.7
  116.8 0.5 fusion.6
  117.3 0.5 fusion.5
  117.7 0.5 fusion.4
  118.2 0.5 fusion.3
  118.7 0.5 fusion.2
  119.2 0.5 fusion.1
  119.7 0.5 fusion
  120.2 0.3 maximum_multiply_fusion
  120.4 0.1 fusion.120
  120.6 16.7 %collective-permute-start = (f32[8,128,256]{2,1,0:T(8,128)S(1)}, f32[8,128,256]{2,1,0:T(8,128)S(1)}, u32[]{:S(2)}, u32[]{:S(2)}) collective-permute-start(f32[8,128,256]{2,1,0:T(8,128)S(1)} %get-tuple-element.11), channel_id=1, source_target_pairs={{32,0},{64,32},{96,64},{128,96},{160,128},{192,160},{224,192},{256... | collective-permute-start | bytes 3145736 | tf_op jit(solution)/shard_map/ppermute | solution.py:18
  137.3 14.5 %collective-permute-done = f32[8,128,256]{2,1,0:T(8,128)S(1)} collective-permute-done((f32[8,128,256]{2,1,0:T(8,128)S(1)}, f32[8,128,256]{2,1,0:T(8,128)S(1)}, u32[]{:S(2)}, u32[]{:S(2)}) %collective-permute-start) | collective-permute-done | bytes 1048608 | tf_op jit(solution)/shard_map/ppermute | solution.py:18
  151.8 0.3 maximum_add_fusion
  152.1 1.1 fusion.17
  153.3 116.3 %all-reduce.2.cloned.1.call-done = f32[8,128,128]{2,1,0:T(8,128)} async-done(((f32[8,128,128]{2,1,0:T(8,128)}), f32[8,128,128]{2,1,0:T(8,128)}) %all-reduce.2.cloned.1.call-update) | async-done | bytes 524304 | tf_op jit(solution)/shard_map/pmax | solution.py:119
  269.6 1.4 constant_dynamic-slice_fusion
  (8 shorter events, 0.2 us)
Async XLA Ops:
  9.8 71.1 %all-to-all-start = ((f32[32,1,128]{2,1,0:T(1,128)}), f32[32,1,128]{2,1,0:T(1,128)S(1)}, u32[]{:S(2)}, u32[]{:S(2)}) async-start(f32[32,1,128]{2,1,0:T(1,128)} %reshape.993), calls=%async_computation | async-start | bytes 32768 | tf_op jit(solution)/shard_map/all_to_all | solution.py:67
  20.3 249.3 %all-reduce.2.cloned.1.call-start = ((), (), s32[]{:S(2)}) async-start(), calls=%async_computation.1 | async-start | bytes 1048576 | tf_op jit(solution)/shard_map/pmax | solution.py:119
  120.6 31.2 %collective-permute-start = (f32[8,128,256]{2,1,0:T(8,128)S(1)}, f32[8,128,256]{2,1,0:T(8,128)S(1)}, u32[]{:S(2)}, u32[]{:S(2)}) collective-permute-start(f32[8,128,256]{2,1,0:T(8,128)S(1)} %get-tuple-element.11), channel_id=1, source_target_pairs={{32,0},{64,32},{96,64},{128,96},{160,128},{192,160},{224,192},{256... | collective-permute-start | bytes 3145736 | tf_op jit(solution)/shard_map/ppermute | solution.py:18
  152.1 118.8 %copy-start = (f32[2,8,128,256]{3,2,1,0:T(8,128)}, f32[2,8,128,256]{3,2,1,0:T(8,128)S(1)}, u32[]{:S(2)}) copy-start(f32[2,8,128,256]{3,2,1,0:T(8,128)S(1)} %maximum_add_fusion) | copy-start | bytes 6291460
Sparse Core Ops, SparseCore 0:
  153.4 116.1 all-reduce.1
